TPU v7x, 32 devices: a whole 2x2x4 slice. The times are simulated.
32 devices in a mesh: cl: 8 (over z, x), grp: 4 (over y, core).
Axes of the slice: x: 2, y: 2, z: 4, core: 2. Of those that a mesh axis runs over, the one named last changes fastest.
Arguments:
- basis: float32 [16, 4, 64, 128], P(None, 'grp', 'cl'), may hold values from -6 to 6
- near_blocks: bfloat16 [4, 64, 4, 128, 128], P('grp', 'cl'), may hold values from -0.25 to 0.25
- near_list: int32 [4, 64, 4], P('grp', 'cl'), may hold values from 0 to 23
- source_basis: bfloat16 [4, 64, 32, 128], P('grp', 'cl'), may hold values from -0.5 to 0.5
- target_basis: bfloat16 [4, 64, 32, 128], P('grp', 'cl'), may hold values from -1 to 1
- coupling: bfloat16 [4, 128, 1024], P('grp', 'cl'), may hold values from -0.75 to 0.75
- far_target: int32 [4, 128], P('grp'), may hold values from 0 to 63, as said below
- far_source: int32 [4, 128], P('grp', 'cl'), may hold values from 0 to 63, as said below
- far_count: int32 [4, 8], P('grp', 'cl'), may hold values from 8 to 16
Outputs:
- next_vector: float32 [4, 64, 128], P('grp', 'cl')
- hessenberg: float32 [17], replicated
Inputs may be any that keep to these rules, and one draw needn't show every extreme that they name: `far_target`: slots are owned in blocks of 16, block d by owner d of the group, whose clusters are d * 8 to (d + 1) * 8 - 1. Except for slot 1 of each owner, a slot's target lies within 16 clusters before or 23 after the owner's first cluster. Slot 1's target is a cluster of owner (d + 4) % 8. `far_source`: except for slot 0 of each owner, a slot's source lies within 80 clusters before or 87 after the owner's first cluster, and where the slot's target obeys the rule above the source differs from it by 16 to 64 clusters. Slot 0's source is a cluster of owner (d + 4) % 8.
All inputs are finite; a program needn't handle non-finite values.
Results may differ from a plain program's by a relative error of at most 0.0039.
Values may be sent and summed in bfloat16 or wider, within the bound.
A program may use at most 64 MiB of HBM per device.

v0:
```python
import jax
import jax.numpy as jnp
from jax import lax
from jax.sharding import PartitionSpec as P


def with_halo(cells, sides, width):
    for axis, dim in sides:
        count = lax.axis_size(axis)
        ends = count - 1
        head = lax.slice_in_dim(cells, 0, width, axis=dim)
        tail = lax.slice_in_dim(cells, cells.shape[dim] - width, cells.shape[dim], axis=dim)
        cells = jnp.concatenate(
            [
                lax.ppermute(tail, axis, [(i, (i + 1) % count) for i in range(ends)]),
                cells,
                lax.ppermute(head, axis, [((i + 1) % count, i) for i in range(ends)]),
            ],
            axis=dim,
        )
    return cells


def on_device(
    basis,
    near_blocks,
    near_list,
    source_basis,
    target_basis,
    coupling,
    far_target,
    far_source,
    far_count,
):
    basis_count = basis.shape[0]
    clusters = basis.shape[2]
    panels_cl = basis.shape[3]
    ranks = source_basis.shape[2]
    block_slots = coupling.shape[1]
    current = basis[basis_count - 1, 0]
    current_bf = current.astype(jnp.bfloat16)
    window = with_halo(current_bf, (("cl", 0),), clusters)
    gathered = window[near_list[0]]
    near_part = jnp.einsum(
        "tkij,tkj->ti", near_blocks[0], gathered, preferred_element_type=jnp.float32
    )
    expansion = jnp.einsum(
        "srp,sp->sr", source_basis[0], current_bf, preferred_element_type=jnp.float32
    ).astype(jnp.bfloat16)
    my_index = lax.axis_index("cl")
    slot_local = jnp.arange(block_slots, dtype=jnp.int32)
    my_sources = far_source[0]
    all_expansion = lax.all_gather(expansion, "cl", axis=0, tiled=True)
    picked = all_expansion[my_sources]
    square_blocks = coupling[0].reshape(block_slots, ranks, ranks)
    live_mask = (slot_local < far_count[0, 0]).astype(jnp.float32)
    contributions = (
        jnp.einsum("bij,bj->bi", square_blocks, picked, preferred_element_type=jnp.float32)
        * live_mask[:, None]
    )
    my_targets = lax.dynamic_slice_in_dim(far_target[0], my_index * block_slots, block_slots)
    row_ids = jnp.arange(clusters * lax.axis_size("cl"), dtype=jnp.int32)
    selector = (row_ids[:, None] == my_targets[None, :]).astype(jnp.float32)
    coupled = lax.psum_scatter(
        jnp.dot(selector, contributions, precision=lax.Precision.HIGHEST),
        "cl",
        scatter_dimension=0,
        tiled=True,
    )
    coupled_bf = coupled.astype(jnp.bfloat16)
    far_part = jnp.einsum(
        "tr,trp->tp", coupled_bf, target_basis[0], preferred_element_type=jnp.float32
    )
    image = 0.5 * current + near_part + far_part
    flat_basis = basis[:, 0].reshape(basis_count, clusters * panels_cl)
    flat_image = image.reshape(-1)
    panels = float(lax.axis_size("cl") * lax.axis_size("grp") * clusters * panels_cl)
    local_products = jnp.dot(flat_basis, flat_image, precision=lax.Precision.HIGHEST)
    gram_local = jnp.dot(flat_basis, flat_basis.T, precision=lax.Precision.HIGHEST)
    products, image_squares, gram_matrix = lax.psum(
        (local_products, jnp.sum(flat_image * flat_image), gram_local), ("cl", "grp")
    )
    projection = products / panels
    remainder = flat_image - jnp.dot(projection, flat_basis, precision=lax.Precision.HIGHEST)
    squares = (
        image_squares
        - 2.0 * jnp.sum(projection * products)
        + jnp.dot(
            projection,
            jnp.dot(gram_matrix, projection, precision=lax.Precision.HIGHEST),
            precision=lax.Precision.HIGHEST,
        )
    )
    new_norm = jnp.sqrt(squares / panels + 1e-06)
    next_vector = (remainder / new_norm).reshape(1, clusters, panels_cl)
    return (next_vector, jnp.concatenate([projection, new_norm[None]]))


def solution(mesh):
    placed = (
        P(None, "grp", "cl", None),
        P("grp", "cl", None, None, None),
        P("grp", "cl", None),
        P("grp", "cl", None, None),
        P("grp", "cl", None, None),
        P("grp", "cl", None),
        P("grp", None),
        P("grp", "cl"),
        P("grp", "cl"),
    )
    return jax.shard_map(
        on_device,
        mesh=mesh,
        in_specs=placed,
        out_specs=(P("grp", "cl", None), P()),
        check_vma=False,
    )
```

profile of v0, /device:TPU:14, one launch (start us, length us, event | category | flops | bytes accessed | tf_op | source)
XLA Modules:
  0.0 122.3 jit_solution(2837860129529427694)
XLA Ops:
  0.6 0.8 fusion.28
  1.4 3.4 %collective-permute-start = (bf16[8,128]{1,0:T(8,128)(2,1)S(1)}, bf16[8,128]{1,0:T(8,128)(2,1)S(1)}, u32[]{:S(2)}, u32[]{:S(2)}) collective-permute-start(bf16[8,128]{1,0:T(8,128)(2,1)S(1)} %get-tuple-element.7), channel_id=1, source_target_pairs={{0,4},{4,8},{8,12},{12,16},{16,20},{20,24},{24,28},{1,5},{5,9},{9,... | collective-permute-start | bytes 6152 | tf_op jit(solution)/shard_map/ppermute | solution.py:15
  4.9 2.4 %collective-permute-start.1 = (bf16[8,128]{1,0:T(8,128)(2,1)S(1)}, bf16[8,128]{1,0:T(8,128)(2,1)S(1)}, u32[]{:S(2)}, u32[]{:S(2)}) collective-permute-start(bf16[8,128]{1,0:T(8,128)(2,1)S(1)} %get-tuple-element.7), channel_id=1, source_target_pairs={{4,0},{8,4},{12,8},{16,12},{20,16},{24,20},{28,24},{5,1},{9,5},{13... | collective-permute-start | bytes 6152 | tf_op jit(solution)/shard_map/ppermute | solution.py:17
  7.3 0.7 copy-done.3
  8.1 1.0 fusion.9
  9.1 25.3 %all_gather.3 = bf16[64,32]{1,0:T(8,128)(2,1)S(1)} all-gather(bf16[8,32]{1,0:T(8,128)(2,1)S(1)} %convert_element_type.22), channel_id=1, replica_groups=mesh['cl'=8,'grp'=4] {'cl'}, dimensions={0}, use_global_device_ids=true | all-gather | bytes 4608 | tf_op jit(solution)/shard_map/all_gather | solution.py:53
  35.3 0.6 copy-done.6
  36.0 0.6 gather_fusion.1
  36.6 0.2 fusion.17
  36.7 0.2 fusion.14
  37.0 31.1 %all-reduce = bf16[64,32]{1,0:T(8,128)(2,1)S(1)} all-reduce(f32[64,32]{1,0:T(8,128)S(1)} %fusion.14), channel_id=2, replica_groups=mesh['cl'=8,'grp'=4] {'cl'}, use_global_device_ids=true, to_apply=%region_0.0.clone | all-reduce | flops 2048 | bytes 12288
  68.1 0.2 convolution_bitcast_fusion
  68.3 0.7 copy-done.7
  69.0 0.6 dynamic-slice.1
  70.4 0.6 gather_fusion
  71.0 0.4 fusion.1
  71.4 0.6 multiply_reduce_fusion
  72.0 0.1 convolution_bitcast_fusion.2
  72.2 45.3 %all-reduce.1 = (f32[16]{0:T(128)S(1)}, f32[]{:T(128)}, f32[16,16]{1,0:T(8,128)S(1)}) all-reduce(f32[16]{0:T(128)S(1)} %convolution_bitcast_fusion.2, f32[]{:T(128)} %get-tuple-element.5, f32[16,16]{1,0:T(8,128)S(1)} %convolution_bitcast_fusion), channel_id=1, replica_groups=mesh['cl'=8,'grp'=4] {'cl','grp'}, use_global_device_ids=true, to_apply=%region_1.0 | all-reduce | flops 273 | bytes 2184 | tf_op jit(solution)/shard_map/psum | solution.py:80
  117.5 0.6 broadcast_multiply_fusion
  118.1 0.2 fusion.4
  118.2 0.8 fusion.3
  121.1 0.6 fusion.21
  121.7 0.6 pad_maximum_fusion.1
  (28 shorter events, 0.6 us)
Async XLA Ops:
  0.6 70.4 %copy-start = (bf16[1,8,4,128,128]{4,3,2,1,0:T(8,128)(2,1)S(1)}, bf16[1,8,4,128,128]{4,3,2,1,0:T(8,128)(2,1)}, u32[]{:S(2)}) copy-start(bf16[1,8,4,128,128]{4,3,2,1,0:T(8,128)(2,1)} %param.10) | copy-start | bytes 3145732
  1.4 69.0 %collective-permute-start = (bf16[8,128]{1,0:T(8,128)(2,1)S(1)}, bf16[8,128]{1,0:T(8,128)(2,1)S(1)}, u32[]{:S(2)}, u32[]{:S(2)}) collective-permute-start(bf16[8,128]{1,0:T(8,128)(2,1)S(1)} %get-tuple-element.7), channel_id=1, source_target_pairs={{0,4},{4,8},{8,12},{12,16},{16,20},{20,24},{24,28},{1,5},{5,9},{9,... | collective-permute-start | bytes 6152 | tf_op jit(solution)/shard_map/ppermute | solution.py:15
  4.9 65.5 %collective-permute-start.1 = (bf16[8,128]{1,0:T(8,128)(2,1)S(1)}, bf16[8,128]{1,0:T(8,128)(2,1)S(1)}, u32[]{:S(2)}, u32[]{:S(2)}) collective-permute-start(bf16[8,128]{1,0:T(8,128)(2,1)S(1)} %get-tuple-element.7), channel_id=1, source_target_pairs={{4,0},{8,4},{12,8},{16,12},{20,16},{24,20},{28,24},{5,1},{9,5},{13... | collective-permute-start | bytes 6152 | tf_op jit(solution)/shard_map/ppermute | solution.py:17
  7.3 0.7 copy-start.3
  8.1 26.3 %copy-start.5 = (s32[1,16]{1,0:T(1,128)S(1)}, s32[1,16]{1,0:T(1,128)}, u32[]{:S(2)}) copy-start(s32[1,16]{1,0:T(1,128)} %param.16) | copy-start | bytes 196
  9.1 25.3 %copy-start.2 = (bf16[1,16,1024]{2,1,0:T(8,128)(2,1)S(1)}, bf16[1,16,1024]{2,1,0:T(8,128)(2,1)}, u32[]{:S(2)}) copy-start(bf16[1,16,1024]{2,1,0:T(8,128)(2,1)} %param.14) | copy-start | bytes 98308
  35.3 0.7 copy-start.6
  36.7 31.4 %copy-start.1 = (f32[16,1,8,128]{3,2,1,0:T(8,128)S(1)}, f32[16,1,8,128]{3,2,1,0:T(8,128)}, u32[]{:S(2)}) copy-start(f32[16,1,8,128]{3,2,1,0:T(8,128)} %param.9) | copy-start | bytes 196612
  37.0 33.3 %copy-start.4 = (bf16[1,8,32,128]{3,2,1,0:T(8,128)(2,1)S(1)}, bf16[1,8,32,128]{3,2,1,0:T(8,128)(2,1)}, u32[]{:S(2)}) copy-start(bf16[1,8,32,128]{3,2,1,0:T(8,128)(2,1)} %param.13) | copy-start | bytes 196612
  68.3 0.7 copy-start.7
where the time goes:
time: 123 us; the launch traced here: 122 us
  blocking collectives  102 us (83%)
  starting transfers between devices  5.83 us (5%)
  local copies, waits for them, and re-layouts  4.96 us (4%)
  between operations  4.13 us (3%)
  matrix products  3.17 us (3%)
  other arithmetic  2.44 us (2%)
    psum x1, blocking collectives, on_device(): lax.psum((local_products, jnp.sum(flat_image * flat_image), gram_local),...  45.3 us
    unnamed x1, blocking collectives  31.1 us
    all_gather x1, blocking collectives, on_device(): all_expansion = lax.all_gather(expansion, 'cl', axis=0, tiled=True)  25.3 us
    ppermute x1, starting transfers between devices, with_halo(): lax.ppermute(tail, axis, [(i, (i + 1) % count) for i in range(ends)])  3.44 us
    unnamed x17, local copies, waits for them, and re-layouts  2.63 us
  transfers between devices with their start and end apart: 2, of which 0 were waited for; matrix products, arithmetic and copies ran while one was open for 3% of the time, Pallas kernels for 0%

commit v1 on v0

--- a/solution.py
+++ b/solution.py
@@ -50,7 +50,10 @@
     my_index = lax.axis_index("cl")
     slot_local = jnp.arange(block_slots, dtype=jnp.int32)
     my_sources = far_source[0]
-    all_expansion = lax.all_gather(expansion, "cl", axis=0, tiled=True)
+    size = lax.axis_size("cl")
+    blocks = jnp.stack([expansion for _ in range(size)])
+    blocks = lax.all_to_all(blocks, "cl", split_axis=0, concat_axis=0)
+    all_expansion = jnp.concatenate(blocks, axis=0)
     picked = all_expansion[my_sources]
     square_blocks = coupling[0].reshape(block_slots, ranks, ranks)
     live_mask = (slot_local < far_count[0, 0]).astype(jnp.float32)

time: 123 us -> 105 us (0.85)
  blocking collectives: 102 us -> 76.6 us
  starting transfers between devices: 5.83 us -> 12 us
    all_gather x1 -> x0, blocking collectives: 25.3 us -> none  [on_device(): all_expansion = lax.all_gather(expansion, 'cl', axis=0, tiled=True)]
    all_to_all x0 -> x1, starting transfers between devices: none -> 6.22 us  [on_device(): blocks = lax.all_to_all(blocks, 'cl', split_axis=0, concat_axis=0)]
    psum x1, blocking collectives: 45.3 us -> 46.7 us  [on_device(): lax.psum((local_products, jnp.sum(flat_image * flat_image), gram_local),...]
    unnamed x17 -> x19, local copies, waits for them, and re-layouts: 2.63 us -> 3.37 us
  transfers between devices with their start and end apart: 2 -> 3, of which waited for: 0 -> 0; matrix products, arithmetic and copies ran while one was open for 3% -> 4% of each run, Pallas kernels for 0% -> 0%
where the time goes in v1:
time: 105 us; the launch traced here: 104 us
  blocking collectives  76.6 us (73%)
  starting transfers between devices  12 us (11%)
  local copies, waits for them, and re-layouts  5.74 us (5%)
  between operations  4.09 us (4%)
  matrix products  3.11 us (3%)
  other arithmetic  2.43 us (2%)
    psum x1, blocking collectives, on_device(): lax.psum((local_products, jnp.sum(flat_image * flat_image), gram_local),...  46.7 us
    unnamed x1, blocking collectives  29.9 us
    all_to_all x1, starting transfers between devices, on_device(): blocks = lax.all_to_all(blocks, 'cl', split_axis=0, concat_axis=0)  6.22 us
    ppermute x1, starting transfers between devices, with_halo(): lax.ppermute(tail, axis, [(i, (i + 1) % count) for i in range(ends)])  3.44 us
    unnamed x19, local copies, waits for them, and re-layouts  3.37 us
    ppermute x1, starting transfers between devices, with_halo(): lax.ppermute(head, axis, [((i + 1) % count, i) for i in range(ends)])  2.39 us
  transfers between devices with their start and end apart: 3, of which 0 were waited for; matrix products, arithmetic and copies ran while one was open for 4% of the time, Pallas kernels for 0%

profile of v1, /device:TPU:14, one launch (start us, length us, event | category | flops | bytes accessed | tf_op | source)
XLA Modules:
  0.0 104.0 jit_solution(4613057538775575945)
XLA Ops:
  0.6 0.8 fusion.28
  1.4 3.4 %collective-permute-start = (bf16[8,128]{1,0:T(8,128)(2,1)S(1)}, bf16[8,128]{1,0:T(8,128)(2,1)S(1)}, u32[]{:S(2)}, u32[]{:S(2)}) collective-permute-start(bf16[8,128]{1,0:T(8,128)(2,1)S(1)} %get-tuple-element.7), channel_id=1, source_target_pairs={{0,4},{4,8},{8,12},{12,16},{16,20},{20,24},{24,28},{1,5},{5,9},{9,... | collective-permute-start | bytes 6152 | tf_op jit(solution)/shard_map/ppermute | solution.py:15
  4.9 2.4 %collective-permute-start.1 = (bf16[8,128]{1,0:T(8,128)(2,1)S(1)}, bf16[8,128]{1,0:T(8,128)(2,1)S(1)}, u32[]{:S(2)}, u32[]{:S(2)}) collective-permute-start(bf16[8,128]{1,0:T(8,128)(2,1)S(1)} %get-tuple-element.7), channel_id=1, source_target_pairs={{4,0},{8,4},{12,8},{16,12},{20,16},{24,20},{28,24},{5,1},{9,5},{13... | collective-permute-start | bytes 6152 | tf_op jit(solution)/shard_map/ppermute | solution.py:17
  7.3 1.0 fusion.9
  8.3 0.7 reshape.125
  9.0 6.2 %all-to-all-start = ((bf16[8,2,128]{2,1,0:T(2,128)(2,1)}), bf16[8,2,128]{2,1,0:T(2,128)(2,1)S(1)}, u32[]{:S(2)}, u32[]{:S(2)}) async-start(bf16[8,2,128]{2,1,0:T(2,128)(2,1)} %reshape.125), calls=%async_computation | async-start | bytes 8192 | tf_op jit(solution)/shard_map/all_to_all | solution.py:55
  15.4 0.6 copy-done.5
  16.7 0.2 convolution_bitcast_fusion
  16.9 0.7 copy-done.6
  17.9 0.6 copy-done.7
  18.5 0.6 dynamic-slice.1
  19.8 0.6 gather_fusion
  20.4 0.4 fusion.1
  20.8 0.6 gather_fusion.1
  21.4 0.2 fusion.17
  21.6 0.2 fusion.14
  21.8 29.9 %all-reduce = bf16[64,32]{1,0:T(8,128)(2,1)S(1)} all-reduce(f32[64,32]{1,0:T(8,128)S(1)} %fusion.14), channel_id=2, replica_groups=mesh['cl'=8,'grp'=4] {'cl'}, use_global_device_ids=true, to_apply=%region_0.0.clone | all-reduce | flops 2048 | bytes 12288
  51.9 0.6 multiply_reduce_fusion
  52.7 46.7 %all-reduce.1 = (f32[16]{0:T(128)S(1)}, f32[]{:T(128)}, f32[16,16]{1,0:T(8,128)S(1)}) all-reduce(f32[16]{0:T(128)S(1)} %convolution_bitcast_fusion.2, f32[]{:T(128)} %get-tuple-element.5, f32[16,16]{1,0:T(8,128)S(1)} %convolution_bitcast_fusion), channel_id=1, replica_groups=mesh['cl'=8,'grp'=4] {'cl','grp'}, use_global_device_ids=true, to_apply=%region_1.0 | all-reduce | flops 273 | bytes 2184 | tf_op jit(solution)/shard_map/psum | solution.py:83
  99.3 0.6 broadcast_multiply_fusion
  99.9 0.2 fusion.4
  100.1 0.8 fusion.3
  102.8 0.6 fusion.21
  103.4 0.6 pad_maximum_fusion.1
  (32 shorter events, 0.9 us)
Async XLA Ops:
  0.6 19.7 %copy-start = (bf16[1,8,4,128,128]{4,3,2,1,0:T(8,128)(2,1)S(1)}, bf16[1,8,4,128,128]{4,3,2,1,0:T(8,128)(2,1)}, u32[]{:S(2)}) copy-start(bf16[1,8,4,128,128]{4,3,2,1,0:T(8,128)(2,1)} %param.10) | copy-start | bytes 3145732
  1.4 18.3 %collective-permute-start = (bf16[8,128]{1,0:T(8,128)(2,1)S(1)}, bf16[8,128]{1,0:T(8,128)(2,1)S(1)}, u32[]{:S(2)}, u32[]{:S(2)}) collective-permute-start(bf16[8,128]{1,0:T(8,128)(2,1)S(1)} %get-tuple-element.7), channel_id=1, source_target_pairs={{0,4},{4,8},{8,12},{12,16},{16,20},{20,24},{24,28},{1,5},{5,9},{9,... | collective-permute-start | bytes 6152 | tf_op jit(solution)/shard_map/ppermute | solution.py:15
  4.9 14.9 %collective-permute-start.1 = (bf16[8,128]{1,0:T(8,128)(2,1)S(1)}, bf16[8,128]{1,0:T(8,128)(2,1)S(1)}, u32[]{:S(2)}, u32[]{:S(2)}) collective-permute-start(bf16[8,128]{1,0:T(8,128)(2,1)S(1)} %get-tuple-element.7), channel_id=1, source_target_pairs={{4,0},{8,4},{12,8},{16,12},{20,16},{24,20},{28,24},{5,1},{9,5},{13... | collective-permute-start | bytes 6152 | tf_op jit(solution)/shard_map/ppermute | solution.py:17
  7.3 7.9 %copy-start.3 = (s32[1,8,4]{1,2,0:T(4,128)S(1)}, s32[1,8,4]{1,2,0:T(4,128)}, u32[]{:S(2)}) copy-start(s32[1,8,4]{1,2,0:T(4,128)} %param.11) | copy-start | bytes 388
  8.3 8.5 %copy-start.1 = (f32[16,1,8,128]{3,2,1,0:T(8,128)S(1)}, f32[16,1,8,128]{3,2,1,0:T(8,128)}, u32[]{:S(2)}) copy-start(f32[16,1,8,128]{3,2,1,0:T(8,128)} %param.9) | copy-start | bytes 196612
  9.0 11.8 %all-to-all-start = ((bf16[8,2,128]{2,1,0:T(2,128)(2,1)}), bf16[8,2,128]{2,1,0:T(2,128)(2,1)S(1)}, u32[]{:S(2)}, u32[]{:S(2)}) async-start(bf16[8,2,128]{2,1,0:T(2,128)(2,1)} %reshape.125), calls=%async_computation | async-start | bytes 8192 | tf_op jit(solution)/shard_map/all_to_all | solution.py:55
  15.4 0.7 copy-start.5
  16.7 1.0 copy-start.2
  16.9 0.7 copy-start.6
  17.8 0.7 copy-start.7
  21.6 30.2 %copy-start.4 = (bf16[1,8,32,128]{3,2,1,0:T(8,128)(2,1)S(1)}, bf16[1,8,32,128]{3,2,1,0:T(8,128)(2,1)}, u32[]{:S(2)}) copy-start(bf16[1,8,32,128]{3,2,1,0:T(8,128)(2,1)} %param.13) | copy-start | bytes 196612
